TPU v7x, 512 devices: a whole 4x8x8 slice. The times are simulated.
512 devices in a mesh: row: 32 (over x, y), col: 16 (over z, core).
Axes of the slice: x: 4, y: 8, z: 8, core: 2. Of those that a mesh axis runs over, the one named last changes fastest.
Arguments:
- features: bfloat16 [131072, 128], P(('row', 'col')), may hold values from -6 to 6
- degree: int32 [131072], P(('row', 'col')), may hold values from 1 to 256
- weight: bfloat16 [128, 128], replicated, may hold values from -0.5 to 0.5
- bias: float32 [128], replicated, may hold values from -3 to 3
- cotangent: bfloat16 [131072, 128], P(('row', 'col')), may hold values from -8 to 8
- tile_rows: int32 [32, 16, 128], P('row', 'col'), may hold values from 0 to 31
- tile_cols: int32 [32, 16, 128], P('row', 'col'), may hold values from 0 to 63
- tile_count: int32 [32, 16, 1], P('row', 'col'), may hold values from 32 to 128, as said below
- tile_codes: int32 [32, 16, 128, 256], P('row', 'col'), may hold values from 0 to 4095
Outputs:
- hidden: bfloat16 [131072, 128], P(('row', 'col'))
- grad_features: bfloat16 [131072, 128], P(('row', 'col'))
- grad_weight: float32 [128, 128], replicated
- grad_bias: float32 [128], replicated
Inputs may be any that keep to these rules, and one draw needn't show every extreme that they name: Only the first tile_count slots of a block are live; on some block the count is exactly 128. `tile_rows`: A tile position may repeat within a block; repeated tiles add.
All inputs are finite; a program needn't handle non-finite values.
Results may differ from a plain program's by a relative error of at most 0.019.
Values may be sent and summed in bfloat16 or wider, within the bound.
A program may use at most 64 MiB of HBM per device.

v0:
```python
import math
import jax
import jax.numpy as jnp
from jax import lax
from jax.sharding import PartitionSpec as P

BLOCK = 16


def tile_mask(code_block, living):
    tile_side = code_block.shape[1] // 2
    row_code = code_block[:, :tile_side][:, :, None]
    col_code = code_block[:, tile_side:][:, None, :]
    hashed = (row_code * col_code + row_code + 3 * col_code) % 4093
    return ((hashed < 64) & living[:, None, None]).astype(jnp.bfloat16)


def accumulate(codes_dev, rows_dev, cols_dev, count_dev, source, out_tiles, backward):
    tile_side = source.shape[1]
    width_feat = source.shape[2]

    def block_step(block_id, summed):
        slot_start = block_id * BLOCK
        code_block = lax.dynamic_slice_in_dim(codes_dev, slot_start, BLOCK, 0)
        row_block = lax.dynamic_slice_in_dim(rows_dev, slot_start, BLOCK, 0)
        col_block = lax.dynamic_slice_in_dim(cols_dev, slot_start, BLOCK, 0)
        slot_ids = slot_start + jnp.arange(BLOCK, dtype=jnp.int32)
        target = col_block if backward else row_block
        anchor = row_block if backward else col_block
        living = slot_ids < count_dev
        keep = tile_mask(code_block, living)
        picked = jnp.take(source, anchor, axis=0)
        if backward:
            product = jnp.einsum("tij,tif->tjf", keep, picked, preferred_element_type=jnp.float32)
        else:
            product = jnp.einsum("tij,tjf->tif", keep, picked, preferred_element_type=jnp.float32)
        return summed.at[target].add(product)

    start_sum = jnp.zeros((out_tiles, tile_side, width_feat), jnp.float32)
    loop_count = codes_dev.shape[0] // BLOCK
    summed = lax.fori_loop(0, loop_count, block_step, start_sum)
    return summed.reshape(out_tiles * tile_side, width_feat)


def dense_part(aggregate, weight, bias, cotangent, inv_root):
    preact = jnp.dot(aggregate, weight, preferred_element_type=jnp.float32) + bias
    hidden = jax.nn.elu(preact).astype(jnp.bfloat16)
    elu_slope = jnp.where(preact > 0, 1.0, jnp.exp(jnp.minimum(preact, 0.0)))
    grad_pre = cotangent.astype(jnp.float32) * elu_slope
    grad_pre_b = grad_pre.astype(jnp.bfloat16)
    grad_weight = lax.dot_general(
        aggregate, grad_pre_b, (((0,), (0,)), ((), ())), preferred_element_type=jnp.float32
    )
    grad_bias = jnp.sum(grad_pre, axis=0)
    grad_agg = jnp.dot(grad_pre_b, weight.T, preferred_element_type=jnp.float32)
    grad_scaled = (inv_root * grad_agg).astype(jnp.bfloat16)
    return (hidden, grad_weight, grad_bias, grad_scaled)


def local(features, degree, weight, bias, cotangent, tile_rows, tile_cols, tile_count, tile_codes):
    codes_dev = tile_codes[0, 0]
    rows_dev = tile_rows[0, 0]
    cols_dev = tile_cols[0, 0]
    count_dev = tile_count[0, 0, 0]
    pieces = features.shape[0]
    width_feat = features.shape[1]
    tile_side = codes_dev.shape[1] // 2
    row_devs = lax.axis_size("row")
    col_devs = lax.axis_size("col")
    grad_scale = 1.0 / math.sqrt(pieces * row_devs * col_devs)
    row_tiles = pieces * col_devs // tile_side
    col_tiles = pieces * row_devs // tile_side
    inv_root = lax.rsqrt(degree.astype(jnp.float32))[:, None]
    scaled = (inv_root * features.astype(jnp.float32)).astype(jnp.bfloat16)
    column_feats = lax.all_gather(scaled, "row", axis=0, tiled=True).reshape(
        col_tiles, tile_side, width_feat
    )
    row_terms = accumulate(codes_dev, rows_dev, cols_dev, count_dev, column_feats, row_tiles, False)
    agg_sum = lax.psum_scatter(
        row_terms.astype(jnp.bfloat16), "col", scatter_dimension=0, tiled=True
    ).astype(jnp.float32)
    aggregate = (inv_root * agg_sum).astype(jnp.bfloat16)
    hidden, grad_weight, grad_bias, grad_scaled = dense_part(
        aggregate, weight, bias, cotangent, inv_root
    )
    grad_weight, grad_bias = lax.psum(
        (grad_weight * grad_scale, grad_bias * grad_scale), ("row", "col")
    )
    row_grads = lax.all_gather(grad_scaled, "col", axis=0, tiled=True)
    row_sources = row_grads.reshape(row_tiles, tile_side, width_feat)
    col_terms = accumulate(codes_dev, rows_dev, cols_dev, count_dev, row_sources, col_tiles, True)
    grad_sum = lax.psum_scatter(
        col_terms.astype(jnp.bfloat16), "row", scatter_dimension=0, tiled=True
    ).astype(jnp.float32)
    grad_features = (inv_root * grad_sum).astype(jnp.bfloat16)
    return (hidden, grad_features, grad_weight, grad_bias)


def solution(mesh):
    placed = (
        P(("row", "col"), None),
        P(("row", "col")),
        P(),
        P(),
        P(("row", "col"), None),
        P("row", "col", None),
        P("row", "col", None),
        P("row", "col", None),
        P("row", "col", None, None),
    )
    return jax.shard_map(
        local,
        mesh=mesh,
        in_specs=placed,
        out_specs=(P(("row", "col"), None), P(("row", "col"), None), P(), P()),
        check_vma=False,
    )
```

profile of v0, /device:TPU:1, one launch (start us, length us, event | category | flops | bytes accessed | tf_op | source)
XLA Modules:
  0.0 838.8 jit_solution(7499523494927583328)
XLA Ops:
  9.6 86.1 %all-gather.3.cloned.1.call-done = bf16[8192,128]{1,0:T(8,128)(2,1)} async-done(((bf16[256,128]{1,0:T(8,128)(2,1)}), bf16[8192,128]{1,0:T(8,128)(2,1)}) %all-gather.3.cloned.1.call-update) | async-done | bytes 2097168 | tf_op jit(solution)/shard_map/all_gather | solution.py:75
  96.0 66.9 %while.30 = (s32[]{:T(128)}, f32[32,128,128]{2,1,0:T(8,128)S(1)}, s32[128]{0:T(128)S(1)}, s32[128,256]{1,0:T(8,128)}, s32[]{:T(128)}, /*index=5*/s32[128]{0:T(12...) while((s32[]{:T(128)}, f32[32,128,128]{2,1,0:T(8,128)S(1)}, ...), condition=%wide.region_2.3_spmd, body=%wide.region_0.2_spmd.sunk | while | flops 70519992 | bytes 5837511 | solution.py:41
  97.5 3.0 gather_fusion
  105.9 3.0 gather_fusion
  114.2 3.0 gather_fusion
  122.6 3.0 gather_fusion
  131.0 3.0 gather_fusion
  139.3 3.0 gather_fusion
  156.1 3.0 gather_fusion
  164.1 61.1 %reduce-scatter.3.cloned.1.call-done = bf16[256,128]{1,0:T(8,128)(2,1)} async-done(((bf16[4096,128]{1,0:T(8,128)(2,1)}), bf16[256,128]{1,0:T(8,128)(2,1)}) %reduce-scatter.3.cloned.1.call-update) | async-done | bytes 65552 | tf_op jit(solution)/shard_map/reduce_scatter | solution.py:79
  227.9 43.0 %all-gather.5.cloned.1.call-done = bf16[4096,128]{1,0:T(8,128)(2,1)} async-done(((bf16[256,128]{1,0:T(8,128)(2,1)}), bf16[4096,128]{1,0:T(8,128)(2,1)}) %all-gather.5.cloned.1.call-update) | async-done | bytes 1048592 | tf_op jit(solution)/shard_map/all_gather | solution.py:89
  273.4 63.9 %while.31 = (s32[]{:T(128)}, f32[64,128,128]{2,1,0:T(8,128)}, s32[128]{0:T(128)S(1)}, s32[128,256]{1,0:T(8,128)}, s32[]{:T(128)}, /*index=5*/s32[128]{0:T(128)S(...) while((s32[]{:T(128)}, f32[64,128,128]{2,1,0:T(8,128)}, ...), condition=%wide.region_6.7_spmd, body=%wide.region_4.6_spmd.sunk | while | flops 70519992 | bytes 5837511 | solution.py:41
  278.0 3.4 scatter_fusion.1
  286.0 3.4 scatter_fusion.1
  293.9 3.4 scatter_fusion.1
  301.9 3.4 scatter_fusion.1
  309.9 3.4 scatter_fusion.1
  317.9 3.4 scatter_fusion.1
  325.9 3.4 scatter_fusion.1
  333.9 3.4 scatter_fusion.1
  337.3 3.9 convert_element_type.62
  341.3 98.5 %psum.15 = f32[128]{0:T(128)} all-reduce(f32[128]{0:T(128)S(1)} %broadcast_multiply_fusion.2), channel_id=1, replica_groups=mesh['row'=32,'col'=16] {'row','col'}, use_global_device_ids=true, to_apply=%region_10.11 | all-reduce | flops 128 | bytes 1024 | tf_op jit(solution)/shard_map/psum | solution.py:86
  440.7 117.3 %reduce-scatter.5.cloned.1.call-done = bf16[256,128]{1,0:T(8,128)(2,1)} async-done(((bf16[8192,128]{1,0:T(8,128)(2,1)}), bf16[256,128]{1,0:T(8,128)(2,1)}) %reduce-scatter.5.cloned.1.call-update) | async-done | bytes 65552 | tf_op jit(solution)/shard_map/reduce_scatter | solution.py:92
  559.6 271.2 %all-reduce.2.cloned.1.call-done = f32[128,128]{1,0:T(8,128)} async-done(((f32[128,128]{1,0:T(8,128)}), f32[128,128]{1,0:T(8,128)}) %all-reduce.2.cloned.1.call-update) | async-done | bytes 65552 | tf_op jit(solution)/shard_map/psum | solution.py:86
  (132 shorter events, 95.1 us)
Async XLA Ops:
  7.2 218.1 %copy-start = (bf16[128,128]{1,0:T(8,128)(2,1)S(1)}, bf16[128,128]{1,0:T(8,128)(2,1)}, u32[]{:S(2)}) copy-start(bf16[128,128]{1,0:T(8,128)(2,1)} %param.15) | copy-start | bytes 98308
  7.2 88.8 %copy-start.3 = (s32[1,1,128]{2,1,0:T(1,128)S(1)}, s32[1,1,128]{2,1,0:T(1,128)}, u32[]{:S(2)}) copy-start(s32[1,1,128]{2,1,0:T(1,128)} %param.19) | copy-start | bytes 1540
  7.2 88.8 %copy-start.2 = (s32[1,1,128]{2,1,0:T(1,128)S(1)}, s32[1,1,128]{2,1,0:T(1,128)}, u32[]{:S(2)}) copy-start(s32[1,1,128]{2,1,0:T(1,128)} %param.18) | copy-start | bytes 1540
  7.2 88.5 %all-gather.3.cloned.1.call-start = ((), (), s32[]{:S(2)}) async-start(), calls=%async_computation.2 | async-start | bytes 2162688 | tf_op jit(solution)/shard_map/all_gather | solution.py:75
  9.5 215.7 %reduce-scatter.3.cloned.1.call-start = ((), (), s32[]{:S(2)}) async-start(), calls=%async_computation.3 | async-start | bytes 1114112 | tf_op jit(solution)/shard_map/reduce_scatter | solution.py:79
  162.9 62.3 %copy-start.4 = (bf16[256,128]{1,0:T(8,128)(2,1)S(1)}, bf16[256,128]{1,0:T(8,128)(2,1)}, u32[]{:S(2)}) copy-start(bf16[256,128]{1,0:T(8,128)(2,1)} %param.17) | copy-start | bytes 196612
  162.9 62.3 %copy-start.6 = (f32[128]{0:T(128)S(1)}, f32[128]{0:T(128)}, u32[]{:S(2)}) copy-start(f32[128]{0:T(128)} %param.16) | copy-start | bytes 1540
  164.1 106.8 %all-gather.5.cloned.1.call-start = ((), (), s32[]{:S(2)}) async-start(), calls=%async_computation.4 | async-start | bytes 1114112 | tf_op jit(solution)/shard_map/all_gather | solution.py:89
  227.8 330.2 %reduce-scatter.5.cloned.1.call-start = ((), (), s32[]{:S(2)}) async-start(), calls=%async_computation.5 | async-start | bytes 2162688 | tf_op jit(solution)/shard_map/reduce_scatter | solution.py:92
  270.9 2.5 copy-start.1
  341.2 98.6 %copy-start.5 = (bf16[256,128]{1,0:T(8,128)(2,1)S(1)}, bf16[256,128]{1,0:T(8,128)(2,1)}, u32[]{:S(2)}) copy-start(bf16[256,128]{1,0:T(8,128)(2,1)} %reduce-scatter.3.cloned.1.call-done) | copy-start | bytes 196612
  341.2 489.6 %all-reduce.2.cloned.1.call-start = ((), (), s32[]{:S(2)}) async-start(), calls=%async_computation.6 | async-start | bytes 131072 | tf_op jit(solution)/shard_map/psum | solution.py:86
Sparse Core Ops, SparseCore 0:
  11.8 83.9 all-gather.2
  164.2 60.9 reduce-scatter.2
  227.9 42.9 all-gather.4
  341.3 216.6 reduce-scatter.4
  563.4 267.3 all-reduce.1
where the time goes:
time: 841 us; the launch traced here: 839 us
  waiting for transfers between devices  579 us (69%)
  blocking collectives  98.5 us (12%)
  other arithmetic  73.3 us (9%)
  matrix products  40.1 us (5%)
  local copies, waits for them, and re-layouts  33.5 us (4%)
  between operations  13.9 us (2%)
    psum x1, waiting for transfers between devices, local(): lax.psum((grad_weight * grad_scale, grad_bias * grad_scale), ('row', 'col'))  271 us
    reduce_scatter x1, waiting for transfers between devices, local(): lax.psum_scatter(col_terms.astype(jnp.bfloat16), 'row', scatter_dimension...  117 us
    psum x1, blocking collectives, local(): lax.psum((grad_weight * grad_scale, grad_bias * grad_scale), ('row', 'col'))  98.5 us
    all_gather x1, waiting for transfers between devices, local(): lax.all_gather(scaled, 'row', axis=0, tiled=True)  86.1 us
    reduce_scatter x1, waiting for transfers between devices, local(): lax.psum_scatter(row_terms.astype(jnp.bfloat16), 'col', scatter_dimension...  61.1 us
    all_gather x1, waiting for transfers between devices, local(): row_grads = lax.all_gather(grad_scaled, 'col', axis=0, tiled=True)  43 us
    scatter-add x16, other arithmetic, block_step(): return summed.at[target].add(product)  39.9 us
    gather x16, local copies, waits for them, and re-layouts, block_step(): picked = jnp.take(source, anchor, axis=0)  29.3 us
  transfers between devices with their start and end apart: 5, of which 5 were waited for; matrix products, arithmetic and copies ran while one was open for 0% of the time, Pallas kernels for 0%

commit v1 on v0

--- a/solution.py
+++ b/solution.py
@@ -5,6 +5,11 @@
 from jax.sharding import PartitionSpec as P
 
 BLOCK = 16
+
+
+def axis_by_axis(array, first, second):
+    half = lax.psum(array, first)
+    return lax.psum(half, second)
 
 
 def tile_mask(code_block, living):
@@ -83,8 +88,8 @@
     hidden, grad_weight, grad_bias, grad_scaled = dense_part(
         aggregate, weight, bias, cotangent, inv_root
     )
-    grad_weight, grad_bias = lax.psum(
-        (grad_weight * grad_scale, grad_bias * grad_scale), ("row", "col")
+    grad_weight, grad_bias = axis_by_axis(
+        (grad_weight * grad_scale, grad_bias * grad_scale), "row", "col"
     )
     row_grads = lax.all_gather(grad_scaled, "col", axis=0, tiled=True)
     row_sources = row_grads.reshape(row_tiles, tile_side, width_feat)

time: 841 us -> 770 us (0.916)
  waiting for transfers between devices: 579 us -> 507 us
    psum x1 -> x2, waiting for transfers between devices: 271 us -> 111 us  [the longest x1 111 us: axis_by_axis(): return lax.psum(half, second)]
    reduce_scatter x1, waiting for transfers between devices: 117 us -> 207 us  [local(): lax.psum_scatter(col_terms.astype(jnp.bfloat16), 'row', scatter_dimension...]
    psum x1 -> x2, blocking collectives: 98.5 us -> 98.5 us  [the longest x1 60.6 us: axis_by_axis(): half = lax.psum(array, first)]
  transfers between devices with their start and end apart: 5 -> 6, of which waited for: 5 -> 5; matrix products, arithmetic and copies ran while one was open for 0% -> 10% of each run, Pallas kernels for 0% -> 0%
where the time goes in v1:
time: 770 us; the launch traced here: 768 us
  waiting for transfers between devices  507 us (66%)
  blocking collectives  98.5 us (13%)
  other arithmetic  73.3 us (10%)
  matrix products  41 us (5%)
  local copies, waits for them, and re-layouts  33.3 us (4%)
  between operations  14.2 us (2%)
    reduce_scatter x1, waiting for transfers between devices, local(): lax.psum_scatter(col_terms.astype(jnp.bfloat16), 'row', scatter_dimension...  207 us
    psum x1, waiting for transfers between devices, axis_by_axis(): return lax.psum(half, second)  111 us
    all_gather x1, waiting for transfers between devices, local(): lax.all_gather(scaled, 'row', axis=0, tiled=True)  86.1 us
    reduce_scatter x1, waiting for transfers between devices, local(): lax.psum_scatter(row_terms.astype(jnp.bfloat16), 'col', scatter_dimension...  61.1 us
    psum x1, blocking collectives, axis_by_axis(): half = lax.psum(array, first)  60.6 us
    all_gather x1, waiting for transfers between devices, local(): row_grads = lax.all_gather(grad_scaled, 'col', axis=0, tiled=True)  41.2 us
    scatter-add x16, other arithmetic, block_step(): return summed.at[target].add(product)  40 us
    psum x1, blocking collectives, axis_by_axis(): return lax.psum(half, second)  37.9 us
  transfers between devices with their start and end apart: 6, of which 5 were waited for; matrix products, arithmetic and copies ran while one was open for 10% of the time, Pallas kernels for 0%

profile of v1, /device:TPU:1, one launch (start us, length us, event | category | flops | bytes accessed | tf_op | source)
XLA Modules:
  0.0 767.9 jit_solution(11202289678529137173)
XLA Ops:
  9.6 86.1 %all-gather.3.cloned.1.call-done = bf16[8192,128]{1,0:T(8,128)(2,1)} async-done(((bf16[256,128]{1,0:T(8,128)(2,1)}), bf16[8192,128]{1,0:T(8,128)(2,1)}) %all-gather.3.cloned.1.call-update) | async-done | bytes 2097168 | tf_op jit(solution)/shard_map/all_gather | solution.py:80
  96.0 66.8 %while.30 = (s32[]{:T(128)}, f32[32,128,128]{2,1,0:T(8,128)S(1)}, s32[128]{0:T(128)S(1)}, s32[128,256]{1,0:T(8,128)}, s32[]{:T(128)}, /*index=5*/s32[128]{0:T(12...) while((s32[]{:T(128)}, f32[32,128,128]{2,1,0:T(8,128)S(1)}, ...), condition=%wide.region_2.3_spmd, body=%wide.region_0.2_spmd.sunk | while | flops 70519992 | bytes 5837511 | solution.py:46
  97.5 3.0 gather_fusion
  105.9 3.0 gather_fusion
  114.2 3.0 gather_fusion
  122.6 3.0 gather_fusion
  130.9 3.0 gather_fusion
  155.9 3.0 gather_fusion
  164.0 61.1 %reduce-scatter.3.cloned.1.call-done = bf16[256,128]{1,0:T(8,128)(2,1)} async-done(((bf16[4096,128]{1,0:T(8,128)(2,1)}), bf16[256,128]{1,0:T(8,128)(2,1)}) %reduce-scatter.3.cloned.1.call-update) | async-done | bytes 65552 | tf_op jit(solution)/shard_map/reduce_scatter | solution.py:84
  229.5 41.2 %all-gather.5.cloned.1.call-done = bf16[4096,128]{1,0:T(8,128)(2,1)} async-done(((bf16[256,128]{1,0:T(8,128)(2,1)}), bf16[4096,128]{1,0:T(8,128)(2,1)}) %all-gather.5.cloned.1.call-update) | async-done | bytes 1048592 | tf_op jit(solution)/shard_map/all_gather | solution.py:94
  273.2 64.0 %while.31 = (s32[]{:T(128)}, f32[64,128,128]{2,1,0:T(8,128)}, s32[128]{0:T(128)S(1)}, s32[128,256]{1,0:T(8,128)}, s32[]{:T(128)}, /*index=5*/s32[128]{0:T(128)S(...) while((s32[]{:T(128)}, f32[64,128,128]{2,1,0:T(8,128)}, ...), condition=%wide.region_6.7_spmd, body=%wide.region_4.6_spmd.sunk | while | flops 70519992 | bytes 5837511 | solution.py:46
  277.8 3.4 scatter_fusion.1
  285.8 3.4 scatter_fusion.1
  293.8 3.4 scatter_fusion.1
  301.7 3.4 scatter_fusion.1
  309.7 3.4 scatter_fusion.1
  317.7 3.4 scatter_fusion.1
  325.8 3.4 scatter_fusion.1
  333.7 3.4 scatter_fusion.1
  337.2 3.9 convert_element_type.62
  341.1 60.6 %psum.30 = f32[128]{0:T(128)S(1)} all-reduce(f32[128]{0:T(128)S(1)} %broadcast_multiply_fusion.2), channel_id=1, replica_groups=mesh['row'=32,'col'=16] {'row'}, use_global_device_ids=true, to_apply=%region_11.12 | all-reduce | flops 128 | bytes 1024 | tf_op jit(solution)/shard_map/psum | solution.py:11
  401.8 37.9 %psum.31 = f32[128]{0:T(128)} all-reduce(f32[128]{0:T(128)S(1)} %psum.30), channel_id=1, replica_groups=mesh['row'=32,'col'=16] {'col'}, use_global_device_ids=true, to_apply=%region_12.13 | all-reduce | flops 128 | bytes 1024 | tf_op jit(solution)/shard_map/psum | solution.py:12
  439.7 207.1 %reduce-scatter.5.cloned.1.call-done = bf16[256,128]{1,0:T(8,128)(2,1)} async-done(((bf16[8192,128]{1,0:T(8,128)(2,1)}), bf16[256,128]{1,0:T(8,128)(2,1)}) %reduce-scatter.5.cloned.1.call-update) | async-done | bytes 65552 | tf_op jit(solution)/shard_map/reduce_scatter | solution.py:97
  648.4 111.2 %all-reduce.5.cloned.1.call-done = f32[128,128]{1,0:T(8,128)} async-done(((f32[128,128]{1,0:T(8,128)}), f32[128,128]{1,0:T(8,128)}) %all-reduce.5.cloned.1.call-update) | async-done | bytes 65552 | tf_op jit(solution)/shard_map/psum | solution.py:12
  (134 shorter events, 99.0 us)
Async XLA Ops:
  7.2 217.9 %copy-start = (bf16[128,128]{1,0:T(8,128)(2,1)S(1)}, bf16[128,128]{1,0:T(8,128)(2,1)}, u32[]{:S(2)}) copy-start(bf16[128,128]{1,0:T(8,128)(2,1)} %param.15) | copy-start | bytes 98308
  7.2 88.8 %copy-start.3 = (s32[1,1,128]{2,1,0:T(1,128)S(1)}, s32[1,1,128]{2,1,0:T(1,128)}, u32[]{:S(2)}) copy-start(s32[1,1,128]{2,1,0:T(1,128)} %param.19) | copy-start | bytes 1540
  7.2 88.8 %copy-start.2 = (s32[1,1,128]{2,1,0:T(1,128)S(1)}, s32[1,1,128]{2,1,0:T(1,128)}, u32[]{:S(2)}) copy-start(s32[1,1,128]{2,1,0:T(1,128)} %param.18) | copy-start | bytes 1540
  7.2 88.5 %all-gather.3.cloned.1.call-start = ((), (), s32[]{:S(2)}) async-start(), calls=%async_computation.2 | async-start | bytes 2162688 | tf_op jit(solution)/shard_map/all_gather | solution.py:80
  9.5 215.5 %reduce-scatter.3.cloned.1.call-start = ((), (), s32[]{:S(2)}) async-start(), calls=%async_computation.3 | async-start | bytes 1114112 | tf_op jit(solution)/shard_map/reduce_scatter | solution.py:84
  162.7 62.3 %copy-start.4 = (bf16[256,128]{1,0:T(8,128)(2,1)S(1)}, bf16[256,128]{1,0:T(8,128)(2,1)}, u32[]{:S(2)}) copy-start(bf16[256,128]{1,0:T(8,128)(2,1)} %param.17) | copy-start | bytes 196612
  162.8 62.3 %copy-start.5 = (f32[128]{0:T(128)S(1)}, f32[128]{0:T(128)}, u32[]{:S(2)}) copy-start(f32[128]{0:T(128)} %param.16) | copy-start | bytes 1540
  163.9 106.8 %all-gather.5.cloned.1.call-start = ((), (), s32[]{:S(2)}) async-start(), calls=%async_computation.4 | async-start | bytes 1114112 | tf_op jit(solution)/shard_map/all_gather | solution.py:94
  227.7 212.0 %all-reduce.3.cloned.1.call-start = ((), (), s32[]{:S(2)}) async-start(), calls=%async_computation.6 | async-start | bytes 131072 | tf_op jit(solution)/shard_map/psum | solution.py:11
  229.5 417.3 %reduce-scatter.5.cloned.1.call-start = ((), (), s32[]{:S(2)}) async-start(), calls=%async_computation.5 | async-start | bytes 2162688 | tf_op jit(solution)/shard_map/reduce_scatter | solution.py:97
  270.7 2.5 copy-start.1
  341.1 418.5 %all-reduce.5.cloned.1.call-start = ((), (), s32[]{:S(2)}) async-start(), calls=%async_computation.7 | async-start | bytes 131072 | tf_op jit(solution)/shard_map/psum | solution.py:12
Sparse Core Ops, SparseCore 0:
  11.8 83.9 all-gather.2
  164.0 60.9 reduce-scatter.2
  227.8 42.9 all-gather.4
  274.6 146.0 all-reduce.2
  424.9 221.7 reduce-scatter.4
  649.0 110.5 all-reduce.4
